TPU v7x, 256 devices: a whole 4x4x8 slice. The times are simulated.
256 devices in a mesh: bead: 64 (over x, z, y_hi), slab: 4 (over y_lo, core).
Axes of the slice: x: 4, y: 4 (y_hi: 2, y_lo: 2; y = y_hi * 2 + y_lo), z: 8, core: 2. Of those that a mesh axis runs over, the one named last changes fastest.
Arguments:
- section: float32 [64, 3, 16384], P('bead', None, 'slab'), may hold values from -0.4 to 12, as said below
- momentum: float32 [64, 3, 16384], P('bead', None, 'slab'), may hold values from -6 to 6
- neighbours: int32 [4, 32, 8], P('slab'), may hold values from 0 to 39
- border_rows: int32 [4, 2, 512], P('slab'), may hold values from 0 to 2047
- counts: int32 [4], P('slab'), may hold values from 2048 to 4096
Outputs:
- new_section: float32 [64, 3, 16384], P('bead', None, 'slab')
- new_momentum: float32 [64, 3, 16384], P('bead', None, 'slab')
Inputs may be any that keep to these rules, and one draw needn't show every extreme that they name: section[0] holds positions whose component 0 lies in its slab's range [3 s, 3 s + 3) and components 1 and 2 in [0, 3); the other beads hold displacements within 0.4. `border_rows`: every listed halo row is below the sending slab's count.
All inputs are finite; a program needn't handle non-finite values.
Results may differ from a plain program's by a relative error of at most 0.0003.
Values sent between devices are 32-bit elements; how exact they have to be, the bound alone decides.
A program may use at most 64 MiB of HBM per device.

v0:
```python
import math
import jax
import jax.numpy as jnp
from jax import lax
from jax.sharding import PartitionSpec as P

time_step = 0.1
omega_sq = 4.0
slab_width = 3.0
cut_sq = 16.0


def broadcast(value, axis, root):
    mine = lax.axis_index(axis) == root
    return lax.psum(jnp.where(mine, value, jnp.zeros_like(value)), axis)


def prefix(value, axis, combine, identity):
    size, index = (lax.axis_size(axis), lax.axis_index(axis))
    everything = lax.all_gather(value, axis)
    start = jnp.broadcast_to(jnp.asarray(identity, value.dtype), value.shape)

    def step(k, before):
        at = size - 1 - k
        reached = at > index
        new = combine(before, everything[at])
        return jnp.where(reached, new, before)

    return lax.fori_loop(0, size, step, start)


def shifted(value, axis, steps):
    count = lax.axis_size(axis)
    pairs = [(source, (source + steps) % count) for source in range(count)]
    return lax.ppermute(value, axis, pairs)


def pair_forces(atom_places, lower, upper, neighbours, count):
    tile = 128
    layer_width = atom_places.shape[1]
    halo = lower.shape[1]
    extended = jnp.concatenate([lower, atom_places, upper], axis=1)
    rows = jnp.arange(extended.shape[1], dtype=jnp.int32)
    live = jnp.logical_or(rows < halo, rows >= halo + layer_width)
    live = jnp.logical_or(live, rows - halo < count)
    ext_mask = live.astype(jnp.float32).reshape(-1, tile)
    ext_tiles = extended.reshape(3, -1, tile)
    tiles = layer_width // tile
    group = math.gcd(tiles, 8)
    own = atom_places.reshape(3, tiles // group, group, tile).transpose(1, 0, 2, 3)
    lists = neighbours.reshape(tiles // group, group, -1)

    def block(item):
        own_block, list_block = item
        partner = ext_tiles[:, list_block].reshape(3, group, -1)
        weight = ext_mask[list_block].reshape(group, -1)
        diff = own_block[:, :, :, None] - partner[:, :, None, :]
        dist = jnp.sum(diff * diff, axis=0)
        inverse = 1.0 / (dist + 1.0)
        inv_two = inverse * inverse
        inv_four = inv_two * inv_two
        inv_seven = inv_four * inv_two * inverse
        cutoff = jnp.maximum(1.0 - dist / cut_sq, 0.0)
        factor = (48.0 * inv_seven - 24.0 * inv_four) * cutoff * cutoff * weight[:, None, :]
        return jnp.sum(diff * factor[None], axis=-1)

    result = lax.map(block, (own, lists))
    force = result.transpose(1, 0, 2, 3).reshape(3, layer_width)
    own_live = (jnp.arange(layer_width, dtype=jnp.int32) < count).astype(jnp.float32)
    return force * own_live[None, :]


def adding(earlier, later):
    return earlier + later


def body(section, momentum, neighbours, border_rows, counts):
    bead_replicas = lax.axis_size("bead")
    level = lax.axis_index("bead").astype(jnp.float32)
    safe_level = jnp.maximum(level, 1.0)
    coords = section[0]
    first = broadcast(coords, "bead", 0)
    scaled = jnp.where(level > 0, coords / safe_level, 0.0)
    suffix = prefix(scaled, "bead", adding, jnp.zeros_like(scaled))
    atom_places = jnp.where(level > 0, first + level * (suffix + scaled), coords)
    slab_layers = lax.axis_size("slab")
    slab_id = lax.axis_index("slab")
    box = slab_width * slab_layers
    first_axis = jnp.array([1.0, 0.0, 0.0], dtype=jnp.float32)[:, None]
    upward_send = atom_places[:, border_rows[0, 0]]
    downward_send = atom_places[:, border_rows[0, 1]]
    lower = shifted(upward_send, "slab", 1)
    upper = shifted(downward_send, "slab", -1)
    lower = lower - jnp.where(slab_id == 0, box, 0.0) * first_axis
    upper = upper + jnp.where(slab_id == slab_layers - 1, box, 0.0) * first_axis
    bead_force = pair_forces(atom_places, lower, upper, neighbours[0], counts[0]) / float(
        bead_replicas
    )
    weighted = level * bead_force
    after = prefix(weighted, "bead", adding, jnp.zeros_like(weighted))
    total, weighted_total = lax.psum((bead_force, weighted), "bead")
    section_force = jnp.where(level > 0, (weighted_total - after) / safe_level, total)
    mass = jnp.where(level > 0, (level + 1.0) / safe_level, 1.0)
    spring = jnp.where(level > 0, omega_sq * mass, 0.0)
    step = time_step / 3.0
    p = momentum[0] + 0.5 * time_step * section_force
    u = coords
    for turn in range(3):
        p = p - 0.5 * step * spring * u
        u = u + step * p / mass
        p = p - 0.5 * step * spring * u
    return (u[None], p[None])


def solution(mesh):
    return jax.shard_map(
        body,
        mesh=mesh,
        in_specs=(
            P("bead", None, "slab"),
            P("bead", None, "slab"),
            P("slab", None, None),
            P("slab", None, None),
            P("slab"),
        ),
        out_specs=(P("bead", None, "slab"), P("bead", None, "slab")),
        check_vma=False,
    )
```

profile of v0, /device:TPU:8, one launch (start us, length us, event | category | flops | bytes accessed | tf_op | source)
XLA Modules:
  0.0 1246.0 jit_solution(6940184823683874336)
XLA Ops:
  7.2 1.5 fusion.20
  11.1 360.9 %psum.21 = f32[3,4096]{1,0:T(4,128)S(1)} all-reduce(f32[3,4096]{1,0:T(4,128)S(1)} %fusion.17), channel_id=1, replica_groups=mesh['bead'=64,'slab'=4] {'bead'}, use_global_device_ids=true, to_apply=%region_0.1 | all-reduce | flops 12288 | bytes 98304 | tf_op jit(solution)/shard_map/psum | solution.py:15
  373.4 59.7 %while.44 = (s32[]{:T(128)}, f32[3,4096]{1,0:T(4,128)S(1)}, s32[]{:T(128)}, f32[64,3,4096]{2,1,0:T(4,128)}, s32[]{:T(128)}, /*index=5*/s32[]{:T(128)}, s32[]{:T(128)}, s32[]{:T(128)}) while((s32[]{:T(128)}, f32[3,4096]{1,0:T(4,128)S(1)}, s32[]{:T(128)}, f32[64,3,4096]{2,1,0:T(4,128)}, s32[]{:T(128)}, /*index=5*/s32[]{:T(128)}, ...), condition=%wide.region_2.3_spmd.clone, body=%wide.region_1.2_spmd.clone.sunk | while | flops 36872 | bytes 147611 | solution.py:29
  434.7 1.0 gather_fusion.3
  435.9 1.0 gather_fusion.2
  437.6 2.5 collective-permute-done
  440.3 42.8 %while.43 = (s32[]{:T(128)}, f32[4,3,8,128]{3,2,1,0:T(8,128)S(1)}, f32[4,3,8,128]{3,2,1,0:T(8,128)S(1)}, s32[4,8,8]{2,1,0:T(8,128)S(1)}, f32[3,40,128]{2,0,1:T(4,128)S(1)}, /*index=5*/s32[]{:T(128)}, s32[]{:T(128)}) while((s32[]{:T(128)}, f32[4,3,8,128]{3,2,1,0:T(8,128)S(1)}, f32[4,3,8,128]{3,2,1,0:T(8,128)S(1)}, ...), condition=%wide.region_6.7_spmd.clone, body=%wide.region_3.6_spmd.clone.sunk | while | flops 33598656 | bytes 17839964 | solution.py:67
  441.1 3.2 fusion.32
  445.6 3.7 fusion.34
  449.3 1.7 fusion.35
  451.8 3.2 fusion.32
  456.3 3.7 fusion.34
  460.0 1.7 fusion.35
  462.5 3.2 fusion.32
  467.0 3.7 fusion.34
  470.7 1.7 fusion.35
  473.3 3.2 fusion.32
  477.7 3.7 fusion.34
  481.4 1.7 fusion.35
  484.7 117.9 %all-gather.5.cloned.1.call-done = f32[64,3,4096]{2,1,0:T(4,128)} async-done(((f32[1,3,4096]{2,1,0:T(4,128)}), f32[64,3,4096]{2,1,0:T(4,128)}) %all-gather.5.cloned.1.call-update) | async-done | bytes 3145744 | tf_op jit(solution)/shard_map/all_gather | solution.py:20
  602.5 59.7 %while.45 = (s32[]{:T(128)}, f32[3,4096]{1,0:T(4,128)S(1)}, s32[]{:T(128)}, f32[64,3,4096]{2,1,0:T(4,128)}, s32[]{:T(128)}, /*index=5*/s32[]{:T(128)}, s32[]{:T(128)}, s32[]{:T(128)}) while((s32[]{:T(128)}, f32[3,4096]{1,0:T(4,128)S(1)}, s32[]{:T(128)}, f32[64,3,4096]{2,1,0:T(4,128)}, s32[]{:T(128)}, /*index=5*/s32[]{:T(128)}, ...), condition=%wide.region_9.10_spmd.clone, body=%wide.region_8.9_spmd.clone.sunk | while | flops 36872 | bytes 147611 | solution.py:29
  622.1 0.9 add_select_fusion.5
  624.9 0.9 add_select_fusion.5
  631.5 0.9 add_select_fusion.5
  633.4 0.9 add_select_fusion.5
  636.2 0.9 add_select_fusion.5
  642.7 0.9 add_select_fusion.5
  644.6 0.9 add_select_fusion.5
  647.4 0.9 add_select_fusion.5
  658.6 0.9 add_select_fusion.5
  662.3 574.8 %all-reduce.3.cloned.1.call-done = (f32[3,4096]{1,0:T(4,128)}, f32[3,4096]{1,0:T(4,128)}) async-done(((f32[3,4096]{1,0:T(4,128)}, f32[3,4096]{1,0:T(4,128)}), (f32[3,4096]{1,0:T(4,128)}, f32[3,4096]{1,0:T(4,128)})) %all-reduce.3.cloned.1.call-update) | async-done | bytes 98320 | tf_op jit(solution)/shard_map/psum | solution.py:101
  1237.1 1.0 subtract_bitcast_fusion
  (202 shorter events, 125.9 us)
Async XLA Ops:
  7.2 366.2 %all-gather.3.cloned.1.call-start = ((), (), s32[]{:S(2)}) async-start(), calls=%async_computation | async-start | bytes 4259840 | tf_op jit(solution)/shard_map/all_gather | solution.py:20
  8.7 593.8 %all-gather.5.cloned.1.call-start = ((), (), s32[]{:S(2)}) async-start(), calls=%async_computation.1 | async-start | bytes 4259840 | tf_op jit(solution)/shard_map/all_gather | solution.py:20
  435.8 1.8 collective-permute-start.1
  437.0 3.1 collective-permute-start
  440.2 796.9 %copy-start = (f32[1,3,4096]{2,0,1:T(1,128)S(1)}, f32[1,3,4096]{2,0,1:T(1,128)}, u32[]{:S(2)}) copy-start(f32[1,3,4096]{2,0,1:T(1,128)} %param.12) | copy-start | bytes 147460
  440.3 796.9 %copy-start.1 = (f32[1,3,4096]{2,0,1:T(1,128)S(1)}, f32[1,3,4096]{2,0,1:T(1,128)}, u32[]{:S(2)}) copy-start(f32[1,3,4096]{2,0,1:T(1,128)} %param.13) | copy-start | bytes 147460
  483.8 753.3 %all-reduce.3.cloned.1.call-start = ((), (), s32[]{:S(2)}) async-start(), calls=%async_computation.2 | async-start | bytes 262144 | tf_op jit(solution)/shard_map/psum | solution.py:101
Sparse Core Ops, SparseCore 0:
  11.5 129.9 all-gather.2
  484.0 118.5 all-gather.4
  605.2 631.8 all-reduce.2
where the time goes:
time: 1250 us
  waiting for transfers between devices  695 us (56%)
  blocking collectives  361 us (29%)
  other arithmetic  161 us (13%)
  between operations  14.6 us (1%)
    psum x1, waiting for transfers between devices, body(): total, weighted_total = lax.psum((bead_force, weighted), 'bead')  575 us
    psum x1, blocking collectives, broadcast(): return lax.psum(jnp.where(mine, value, jnp.zeros_like(value)), axis)  361 us
    all_gather x2, waiting for transfers between devices, prefix(): everything = lax.all_gather(value, axis)  118 us
    select_n x128, other arithmetic, step(): return jnp.where(reached, new, before)  117 us
  transfers between devices with their start and end apart: 5, of which 3 were waited for; matrix products, arithmetic and copies ran while one was open for 5% of the time, Pallas kernels for 0%

commit v1 on v0

--- a/solution.py
+++ b/solution.py
@@ -8,11 +8,12 @@
 omega_sq = 4.0
 slab_width = 3.0
 cut_sq = 16.0
+arrange_pieces_all = lambda values, chip_axis: jnp.sum(lax.all_gather(values, chip_axis), axis=0)
 
 
 def broadcast(value, axis, root):
     mine = lax.axis_index(axis) == root
-    return lax.psum(jnp.where(mine, value, jnp.zeros_like(value)), axis)
+    return arrange_pieces_all(jnp.where(mine, value, jnp.zeros_like(value)), axis)
 
 
 def prefix(value, axis, combine, identity):

time: 1250 us -> 1090 us (0.87)
  blocking collectives: 361 us -> 0 us
  waiting for transfers between devices: 695 us -> 897 us
    psum x1 -> x0, blocking collectives: 361 us -> none  [broadcast(): return lax.psum(jnp.where(mine, value, jnp.zeros_like(value)), axis)]
    all_gather x2, waiting for transfers between devices: 118 us -> 252 us  [prefix(): everything = lax.all_gather(value, axis)]
    all_gather x0 -> x1, waiting for transfers between devices: none -> 67.8 us  [lax.all_gather(values, chip_axis)]
  transfers between devices with their start and end apart: 5 -> 6, of which waited for: 3 -> 5; matrix products, arithmetic and copies ran while one was open for 5% -> 11% of each run, Pallas kernels for 0% -> 0%
where the time goes in v1:
time: 1090 us
  waiting for transfers between devices  897 us (82%)
  other arithmetic  163 us (15%)
  between operations  14.6 us (1%)
    psum x1, waiting for transfers between devices, body(): total, weighted_total = lax.psum((bead_force, weighted), 'bead')  575 us
    all_gather x2, waiting for transfers between devices, prefix(): everything = lax.all_gather(value, axis)  252 us
    select_n x128, other arithmetic, step(): return jnp.where(reached, new, before)  117 us
    all_gather x1, waiting for transfers between devices, lax.all_gather(values, chip_axis)  67.8 us
  transfers between devices with their start and end apart: 6, of which 5 were waited for; matrix products, arithmetic and copies ran while one was open for 11% of the time, Pallas kernels for 0%

profile of v1, /device:TPU:8, one launch (start us, length us, event | category | flops | bytes accessed | tf_op | source)
XLA Modules:
  0.0 1088.6 jit_solution(6608685566743474352)
XLA Ops:
  7.2 1.5 fusion.19
  12.5 128.3 %all-gather.6.cloned.1.call-done = f32[64,3,4096]{2,1,0:T(4,128)} async-done(((f32[1,3,4096]{2,1,0:T(4,128)}), f32[64,3,4096]{2,1,0:T(4,128)}) %all-gather.6.cloned.1.call-update) | async-done | bytes 3145744 | tf_op jit(solution)/shard_map/all_gather | solution.py:21
  140.8 59.7 %while.44 = (s32[]{:T(128)}, f32[3,4096]{1,0:T(4,128)S(1)}, s32[]{:T(128)}, f32[64,3,4096]{2,1,0:T(4,128)}, s32[]{:T(128)}, /*index=5*/s32[]{:T(128)}, s32[]{:T(128)}, s32[]{:T(128)}) while((s32[]{:T(128)}, f32[3,4096]{1,0:T(4,128)S(1)}, s32[]{:T(128)}, f32[64,3,4096]{2,1,0:T(4,128)}, s32[]{:T(128)}, /*index=5*/s32[]{:T(128)}, ...), condition=%wide.region_2.3_spmd.clone, body=%wide.region_1.2_spmd.clone.sunk | while | flops 36872 | bytes 147611 | solution.py:30
  153.8 0.9 add_select_fusion.4
  154.8 0.9 add_select_fusion.4
  155.7 0.9 add_select_fusion.4
  196.8 0.9 add_select_fusion.4
  200.5 67.8 %all-gather.4.cloned.1.call-done = f32[64,3,4096]{2,1,0:T(4,128)} async-done(((f32[1,3,4096]{2,1,0:T(4,128)}), f32[64,3,4096]{2,1,0:T(4,128)}) %all-gather.4.cloned.1.call-update) | async-done | bytes 3145744 | tf_op jit(solution)/shard_map/all_gather | solution.py:11
  268.3 2.8 reduce_sum.27
  271.9 1.0 gather_fusion.3
  273.1 1.0 gather_fusion.2
  274.9 2.5 collective-permute-done
  277.5 42.8 %while.43 = (s32[]{:T(128)}, f32[4,3,8,128]{3,2,1,0:T(8,128)S(1)}, f32[4,3,8,128]{3,2,1,0:T(8,128)S(1)}, s32[4,8,8]{2,1,0:T(8,128)S(1)}, f32[3,40,128]{2,0,1:T(4,128)S(1)}, /*index=5*/s32[]{:T(128)}, s32[]{:T(128)}) while((s32[]{:T(128)}, f32[4,3,8,128]{3,2,1,0:T(8,128)S(1)}, f32[4,3,8,128]{3,2,1,0:T(8,128)S(1)}, ...), condition=%wide.region_6.7_spmd.clone, body=%wide.region_3.6_spmd.clone.sunk | while | flops 33598656 | bytes 17839964 | solution.py:68
  278.3 3.2 fusion.31
  282.8 3.7 fusion.33
  286.5 1.7 fusion.34
  289.0 3.2 fusion.31
  293.5 3.7 fusion.33
  297.2 1.7 fusion.34
  299.7 3.2 fusion.31
  304.2 3.7 fusion.33
  307.9 1.7 fusion.34
  310.4 3.2 fusion.31
  314.9 3.7 fusion.33
  318.6 1.7 fusion.34
  321.9 123.3 %all-gather.8.cloned.1.call-done = f32[64,3,4096]{2,1,0:T(4,128)} async-done(((f32[1,3,4096]{2,1,0:T(4,128)}), f32[64,3,4096]{2,1,0:T(4,128)}) %all-gather.8.cloned.1.call-update) | async-done | bytes 3145744 | tf_op jit(solution)/shard_map/all_gather | solution.py:21
  445.2 59.7 %while.45 = (s32[]{:T(128)}, f32[3,4096]{1,0:T(4,128)S(1)}, s32[]{:T(128)}, f32[64,3,4096]{2,1,0:T(4,128)}, s32[]{:T(128)}, /*index=5*/s32[]{:T(128)}, s32[]{:T(128)}, s32[]{:T(128)}) while((s32[]{:T(128)}, f32[3,4096]{1,0:T(4,128)S(1)}, s32[]{:T(128)}, f32[64,3,4096]{2,1,0:T(4,128)}, s32[]{:T(128)}, /*index=5*/s32[]{:T(128)}, ...), condition=%wide.region_9.10_spmd.clone, body=%wide.region_8.9_spmd.clone.sunk | while | flops 36872 | bytes 147611 | solution.py:30
  456.4 0.9 add_select_fusion.5
  463.0 0.9 add_select_fusion.5
  468.6 0.9 add_select_fusion.5
  505.0 574.7 %all-reduce.3.cloned.1.call-done = (f32[3,4096]{1,0:T(4,128)}, f32[3,4096]{1,0:T(4,128)}) async-done(((f32[3,4096]{1,0:T(4,128)}, f32[3,4096]{1,0:T(4,128)}), (f32[3,4096]{1,0:T(4,128)}, f32[3,4096]{1,0:T(4,128)})) %all-reduce.3.cloned.1.call-update) | async-done | bytes 98320 | tf_op jit(solution)/shard_map/psum | solution.py:102
  1079.7 1.0 subtract_bitcast_fusion
  (204 shorter events, 126.8 us)
Async XLA Ops:
  7.2 264.0 %copy-start = (f32[1,3,4096]{2,0,1:T(1,128)S(1)}, f32[1,3,4096]{2,0,1:T(1,128)}, u32[]{:S(2)}) copy-start(f32[1,3,4096]{2,0,1:T(1,128)} %param.12) | copy-start | bytes 147460
  7.2 133.6 %all-gather.6.cloned.1.call-start = ((), (), s32[]{:S(2)}) async-start(), calls=%async_computation.1 | async-start | bytes 4259840 | tf_op jit(solution)/shard_map/all_gather | solution.py:21
  8.8 259.6 %all-gather.4.cloned.1.call-start = ((), (), s32[]{:S(2)}) async-start(), calls=%async_computation | async-start | bytes 4259840 | tf_op jit(solution)/shard_map/all_gather | solution.py:11
  9.5 435.7 %all-gather.8.cloned.1.call-start = ((), (), s32[]{:S(2)}) async-start(), calls=%async_computation.2 | async-start | bytes 4259840 | tf_op jit(solution)/shard_map/all_gather | solution.py:21
  273.0 1.8 collective-permute-start.1
  274.2 3.1 collective-permute-start
  277.5 802.2 %copy-start.1 = (f32[1,3,4096]{2,0,1:T(1,128)S(1)}, f32[1,3,4096]{2,0,1:T(1,128)}, u32[]{:S(2)}) copy-start(f32[1,3,4096]{2,0,1:T(1,128)} %param.13) | copy-start | bytes 147460
  321.0 758.6 %all-reduce.3.cloned.1.call-start = ((), (), s32[]{:S(2)}) async-start(), calls=%async_computation.3 | async-start | bytes 262144 | tf_op jit(solution)/shard_map/psum | solution.py:102
Sparse Core Ops, SparseCore 0:
  11.5 129.2 all-gather.5
  144.3 124.0 all-gather.3
  321.1 124.0 all-gather.7
  447.8 631.8 all-reduce.2
